TPU v7x, 32 devices: a whole 2x2x4 slice. The times are simulated.
32 devices in a mesh: xy: 8 (over y, x, core), gz: 4 (over z).
Axes of the slice: x: 2, y: 2, z: 4, core: 2. Of those that a mesh axis runs over, the one named last changes fastest.
Arguments:
- velocity: float32 [3, 16, 256, 1024], P(None, 'gz', 'xy'), may hold values from -6 to 6
- magnetic: float32 [3, 8, 128, 512], P(None, 'gz', 'xy'), may hold values from -6 to 6
- slot_block_table: int32 [256], P('xy'), may hold values from 0 to 255, as said below
Outputs:
- updated_fine_velocity: float32 [3, 16, 256, 1024], P(None, 'gz', 'xy')
- magnetic_next: float32 [3, 8, 128, 512], P(None, 'gz', 'xy')
Inputs may be any that keep to these rules, and one draw needn't show every extreme that they name: `slot_block_table`: each block number appears in one slot; the 32 slots of one device along xy hold exactly 4 blocks of every block row.
All inputs are finite; a program needn't handle non-finite values.
Results may differ from a plain program's by a relative error of at most 0.00005.
Values sent between devices are 32-bit elements; how exact they have to be, the bound alone decides.
No kernel may reach another device: no remote copies, remote signals or barrier semaphores. Data moves between devices by JAX's collectives and lax.ppermute only.
A program may use at most 64 MiB of HBM per device.

v0:
```python
import functools
import math

import jax
import jax.numpy as jnp
from jax import lax
from jax.experimental import pallas as pl
from jax.experimental.pallas import tpu as pltpu
from jax.sharding import PartitionSpec as P

F32, BF16 = jnp.float32, jnp.bfloat16
VMEM = pl.BlockSpec(memory_space=pltpu.VMEM)
ALL_VMEM = 67043328
HBM = pl.BlockSpec(memory_space=pltpu.HBM)


def split(x):
    hi = x.astype(BF16)
    return hi, (x - hi.astype(F32)).astype(BF16)


def dot(a, b):
    return jnp.dot(a, b, preferred_element_type=F32)


def iota(shape, dim):
    return lax.broadcasted_iota(jnp.int32, shape, dim)


def one_hot(mask):
    return jnp.where(mask, 1.0, 0.0).astype(BF16)


def log2(x):
    assert x == 1 << (x.bit_length() - 1)
    return x.bit_length() - 1


class Plan:
    def __init__(self, vshape, bshape, n):
        self.n = n
        self.slots = vshape[2]
        self.k = self.slots // n
        self.zc = bshape[1]
        self.ny, self.nx = bshape[2:]
        self.edge = math.isqrt(vshape[3])
        self.half = self.edge // 2
        self.area = self.half * self.half
        self.bcols = self.nx // self.half
        self.rc = -(-self.zc * self.k // 8) * 8
        self.ru = 3 * self.rc
        self.rows = n * self.rc
        self.rb = 3 * self.zc * self.nx // self.area
        self.r1 = -(-(self.ru + self.rb + 4) // 8) * 8
        self.wrap = self.nx // self.area
        assert self.rc == 8 and self.area == 256 and self.half == 16


def mirror(i):
    return (i & ~7) | ((8 - (i & 7)) & 7)


def send_positions(p, table):
    s = p.slots
    row = jnp.broadcast_to((table >> log2(p.bcols)).astype(F32), (s, s))
    i, j = iota((s, s), 0), iota((s, s), 1)
    row_s = jnp.sum(jnp.where(i == j, row, 0.0), axis=1, keepdims=True)
    rank = jnp.sum(jnp.where((row_s == row) & (i < j), 1.0, 0.0), axis=0, keepdims=True)
    q = row[0:1] * p.k + rank
    q_s = jnp.sum(jnp.where(i == j, jnp.broadcast_to(q, (s, s)), 0.0), axis=1, keepdims=True)
    return q, q_s


def select(g, x):
    hi, lo = split(x)
    out = dot(g, jnp.concatenate([hi, lo], axis=1))
    return out[:, : x.shape[1]] + out[:, x.shape[1] :]


def spin(t):
    return pltpu.roll(t, 0, 1, stride=16, stride_axis=0)


def lay_out(t, first):
    t = spin(t)
    here = (iota(t.shape, 1) >> 4) == ((iota(t.shape, 0) + first) & 7)
    return jnp.sum(jnp.where(here, t, 0.0), axis=0, keepdims=True)


def tile_lanes(x, width):
    return x[:, :width] if width <= 128 else jnp.concatenate([x] * (width // 128), axis=1)


def lane_route(p):
    lane = iota((1, 1, p.rows), 2)
    i = lane & (p.rc - 1)
    return lane >> log2(p.rc), i >> log2(p.k), i & (p.k - 1)


def restrict_kernel(p, v_hbm, t_hbm, b_hbm, out_hbm, up_hbm, down_hbm, v_ref, t_ref, b_ref, out, last, first, sems):
    n, k, s, zc = p.n, p.k, p.slots, p.zc
    me = lax.axis_index("xy")
    t_copy = pltpu.make_async_copy(t_hbm, t_ref, sems.at[0])
    b_copy = pltpu.make_async_copy(b_hbm, b_ref, sems.at[1])
    v_copies = [pltpu.make_async_copy(v_hbm.at[c], v_ref.at[c], sems.at[2 + c]) for c in range(3)]
    t_copy.start()
    for copy in v_copies:
        copy.start()
    b_copy.start()
    half_fine = p.edge * p.edge // 2
    half_area = p.area // 2
    f, c = iota((half_fine, half_area), 0), iota((half_fine, half_area), 1)
    e = log2(p.edge)
    coarse = (mirror(f >> (e + 1)) << (e - 1)) + ((f & (p.edge - 1)) >> 1)
    sel = one_hot(coarse == c)
    t_copy.wait()
    table = t_ref[...]
    q, _ = send_positions(p, table)
    lanes = zc * s
    rep = one_hot((iota((s, lanes), 1) & (s - 1)) == iota((s, lanes), 0))
    qt = dot(jnp.broadcast_to(q, (8, s)).astype(BF16), rep)[0:1]
    shape = (n, p.rc, lanes)
    i = iota(shape, 1)
    target = (iota(shape, 0) * k + (i & (k - 1))).astype(F32)
    g = one_hot(((i >> log2(k)) == (iota(shape, 2) >> log2(s))) & (target == qt.reshape(1, 1, lanes)))
    g = g.reshape(p.rows, lanes)
    col = jnp.broadcast_to((table & (p.bcols - 1)).astype(F32), (s, s))
    qi = iota((s, s), 0).astype(F32)
    col_q = jnp.sum(jnp.where(qi == jnp.broadcast_to(q, (s, s)), col, 0.0), axis=1, keepdims=True)
    qa, la = iota((s, p.area), 0), iota((s, p.area), 1)
    place = jnp.where(la < 128, la, jnp.where(la < 192, -la, -1 - la)) & (k - 1)
    spread = jnp.where((qa & (k - 1)) == place, col_q, 0.0).astype(BF16)
    gather = one_hot((iota((n, s), 1) >> log2(k)) == iota((n, s), 0))
    cols = dot(gather, spread)
    at = p.ru + p.rb
    for r in range(n):
        north, south = (r + 1) % n, (r - 1) % n
        out[r, at : at + 1, :128] = cols[r : r + 1, :128]
        outer = jnp.where(iota((1, 128), 1) < 64, cols[north : north + 1, 128:], cols[south : south + 1, 128:])
        out[r, at : at + 1, 128:] = outer
    averages = []
    m = zc * s
    ws = [slice(h * half_fine, (h + 1) * half_fine) for h in range(2)]
    for c in range(3):
        v_copies[c].wait()
        u = []
        for w in ws:
            z_sum = [v_ref[c, 2 * z, :, w] + v_ref[c, 2 * z + 1, :, w] for z in range(zc)]
            o = dot(jnp.concatenate(split(jnp.concatenate(z_sum, axis=0)), axis=0), sel)
            u.append(o[:m] + o[m:])
        averages.append(jnp.concatenate(u, axis=1) * 0.125)
    b_copy.wait()
    sends = [
        pltpu.make_async_copy(b_ref.at[0:2, zc - 1], up_hbm, sems.at[5]),
        pltpu.make_async_copy(b_ref.at[0:2, 0], down_hbm, sems.at[6]),
    ]
    for c in range(3):
        for z in range(zc):
            for h in range(p.wrap):
                at = (c * zc + z) * p.wrap + h
                w = slice(h * p.area, (h + 1) * p.area)
                last[at : at + 1, :] = b_ref[c, z, p.ny - 1 : p.ny, w]
                first[at : at + 1, :] = b_ref[c, z, 0:1, w]
    nxt = lax.rem(me + 1, n)
    for r in range(n):
        out[r, p.ru : p.ru + p.rb, :] = jnp.where(r == nxt, last[: p.rb], first[: p.rb])
    early = pl.ds(p.ru, 8)
    sends.append(pltpu.make_async_copy(out.at[:, early, :], out_hbm.at[:, early, :], sems.at[7]))
    for send in sends:
        send.start()
    for c in range(3):
        blocks = select(g, averages[c])
        out[:, c * p.rc : (c + 1) * p.rc, :] = blocks.reshape(n, p.rc, p.area)
        rows = pl.ds(c * p.rc, p.rc)
        sends.append(pltpu.make_async_copy(out.at[:, rows, :], out_hbm.at[:, rows, :], sems.at[8 + c]))
        sends[-1].start()
        at = p.ru + p.rb + 1 + c
        for r in range(n):
            tile = blocks[r * p.rc : (r + 1) * p.rc]
            out[(r - 1) % n, at : at + 1, :128] = lay_out(tile[:, :128], 0)
            out[(r + 1) % n, at : at + 1, 128:] = lay_out(tile[:, 128:], 1)
    late = pl.ds(p.ru + 8, p.r1 - p.ru - 8)
    sends.append(pltpu.make_async_copy(out.at[:, late, :], out_hbm.at[:, late, :], sems.at[11]))
    sends[-1].start()
    for send in sends:
        send.wait()


def tile_transpose(p, t):
    g = iota(t.shape, 1) >> log2(p.half)
    t = pltpu.roll(t, 0, 1, stride=p.half, stride_axis=0)
    for b in (1, 2, 4):
        t = jnp.where((g & b) != 0, pltpu.roll(t, 8 - b, 0), t)
    return pltpu.roll(t, 0, 1, stride=p.half, stride_axis=0)


def blocks_to_grid(p, blk):
    rows = []
    for yh in range(p.half // 8):
        rows.append(
            jnp.concatenate(
                [
                    tile_transpose(p, blk[8 * c : 8 * c + 8, 128 * yh : 128 * yh + 128])
                    for c in range(p.bcols // 8)
                ],
                axis=1,
            )
        )
    return jnp.concatenate(rows, axis=0)


def grid_to_blocks(p, grid):
    rows = []
    for c in range(p.bcols // 8):
        rows.append(
            jnp.concatenate(
                [
                    tile_transpose(p, grid[8 * yh : 8 * yh + 8, 128 * c : 128 * c + 128])
                    for yh in range(p.half // 8)
                ],
                axis=1,
            )
        )
    return jnp.concatenate(rows, axis=0)


def x_next(f):
    return pltpu.roll(f, f.shape[1] - 1, 1)


def x_prev(f):
    return pltpu.roll(f, 1, 1)


def y_next(f, halo):
    return jnp.where(iota(f.shape, 0) == f.shape[0] - 1, halo, pltpu.roll(f, f.shape[0] - 1, 0))


def y_prev(f, halo):
    return jnp.where(iota(f.shape, 0) == 0, halo, pltpu.roll(f, 1, 0))


def row_of(p, ref, src, at):
    return jnp.concatenate([ref[src, pl.ds(at + h, 1), :] for h in range(p.wrap)], axis=1)


def interior_kernel(p, b_ref, t_ref, copy_ref, j_ref, next_ref, g3_ref):
    s, k = p.slots, p.k
    _, q_s = send_positions(p, t_ref[...])
    r_l, z_l, j_l = lane_route(p)
    shape = (p.zc, s, p.rows)
    g3 = (iota(shape, 0) == z_l) & (q_s.reshape(1, s, 1) == (r_l * k + j_l).astype(F32))
    g3_ref[...] = one_hot(g3).reshape(p.zc * s, p.rows)
    zero = jnp.zeros((p.ny, p.nx), F32)
    for z in range(p.zc):
        b = [b_ref[c, z] for c in range(3)]
        below = [b_ref[c, z - 1] if z > 0 else zero for c in range(3)]
        above = [b_ref[c, z + 1] if z < p.zc - 1 else zero for c in range(3)]
        south, north = [y_prev(f, 0.0) for f in b], [y_next(f, 0.0) for f in b]
        west, east = [x_prev(f) for f in b], [x_next(f) for f in b]
        j_ref[0, z] = ((north[2] - south[2]) - (above[1] - below[1])) * 0.5
        j_ref[1, z] = ((above[0] - below[0]) - (east[2] - west[2])) * 0.5
        j_ref[2, z] = ((east[1] - west[1]) - (north[0] - south[0])) * 0.5
        for c in range(3):
            lap = below[c] + above[c] + south[c] + north[c] + west[c] + east[c] - 6.0 * b[c]
            next_ref[c, z] = b[c] + 0.05 * lap
            copy_ref[c, z] = b[c]


def edge_rows(p, ref, nxt, prv, at):
    y = iota((p.ny, p.nx), 0)
    north = jnp.where(y == p.ny - 1, row_of(p, ref, nxt, at), 0.0)
    return north, jnp.where(y == 0, row_of(p, ref, prv, at), 0.0)


def field_kernel(p, r_ref, b_ref, j_ref, lo_ref, hi_ref, out, e_ref, up_ref, down_ref):
    n, k, zc = p.n, p.k, p.zc
    me = lax.axis_index("xy")
    nxt, prv = lax.rem(me + 1, n), lax.rem(me + n - 1, n)
    b = [[b_ref[c, z] for z in range(zc)] for c in range(3)]
    cols = r_ref[:, p.ru + p.rb, :]
    shape = (n, p.rc, 128)
    col_s = jnp.sum(
        jnp.where((iota(shape, 1) & (k - 1)) == iota(shape, 2), cols[:, None, :128], 0.0), axis=2, keepdims=True
    )
    shape = (n, p.rc, zc * p.bcols)
    lane = iota(shape, 2)
    g = one_hot(
        ((iota(shape, 1) >> log2(k)) == (lane >> log2(p.bcols)))
        & (col_s == mirror(lane & (p.bcols - 1)).astype(F32))
    ).reshape(p.rows, zc * p.bcols)
    force = []
    zero = jnp.zeros((p.ny, p.nx), F32)
    for z in range(zc):
        bz = [b[c][z] for c in range(3)]
        dy = {}
        for c in (0, 2):
            north, south = edge_rows(p, r_ref, nxt, prv, p.ru + (c * zc + z) * p.wrap)
            dy[c] = north - south
        dz = [zero, zero]
        for c in range(2):
            if z == zc - 1:
                dz[c] = dz[c] + hi_ref[c]
            if z == 0:
                dz[c] = dz[c] - lo_ref[c]
        j0 = j_ref[0, z] + (dy[2] - dz[1]) * 0.5
        j1 = j_ref[1, z] + dz[0] * 0.5
        j2 = j_ref[2, z] - dy[0] * 0.5
        force.append([j1 * bz[2] - j2 * bz[1], j2 * bz[0] - j0 * bz[2], j0 * bz[1] - j1 * bz[0]])
    for c in range(3):
        f_blk = jnp.concatenate([grid_to_blocks(p, force[z][c]) for z in range(zc)], axis=0)
        out[:, c * p.rc : (c + 1) * p.rc, :] = select(g, f_blk).reshape(n, p.rc, p.area)
    p_l, z_l, _ = lane_route(p)
    shape = (n, p.rows)
    col_l = jnp.sum(
        jnp.where(iota(shape, 0) == p_l.reshape(1, p.rows), tile_lanes(cols[:, :128], p.rows), 0.0), axis=0, keepdims=True
    )
    shape = (zc, p.bcols, p.rows)
    g = one_hot(
        (iota(shape, 0) == z_l) & (iota(shape, 1).astype(F32) == col_l.reshape(1, 1, p.rows))
    ).reshape(zc * p.bcols, p.rows)
    u = []
    for c in range(3):
        blk = select(g, r_ref[:, c * p.rc : (c + 1) * p.rc, :].reshape(p.rows, p.area))
        u.append([blocks_to_grid(p, blk[z * p.bcols : (z + 1) * p.bcols]) for z in range(zc)])
    for z in range(zc):
        uz, bz = [u[c][z] for c in range(3)], [b[c][z] for c in range(3)]
        ez = [uz[1] * bz[2] - uz[2] * bz[1], uz[2] * bz[0] - uz[0] * bz[2], uz[0] * bz[1] - uz[1] * bz[0]]
        for c in range(3):
            e_ref[c, z] = ez[c]
        if z == zc - 1:
            up_ref[0], up_ref[1], up_ref[2] = ez[0], ez[1], bz[2]
        if z == 0:
            down_ref[0], down_ref[1], down_ref[2] = ez[0], ez[1], bz[2]


def outer_velocity(p, r_ref):
    n, zc = p.n, p.zc
    at = p.ru + p.rb
    x = r_ref[:, at, :][:, 128:]
    spun = pltpu.roll(x, 64, 1)
    low = iota(x.shape, 1) < 64
    lane = iota((1, 1, p.rows), 2)
    place = lane & 7
    shape = (zc, p.bcols, p.rows)
    sides = []
    for d, (cols, i) in enumerate(((jnp.where(low, x, spun), (8 - place) & 7), (jnp.where(low, spun, x), 7 - place))):
        device = iota((n, p.rows), 0) == (lane >> 3).reshape(1, p.rows)
        col = jnp.sum(jnp.where(device, tile_lanes(cols, p.rows), 0.0), axis=0, keepdims=True)
        g = one_hot(
            (iota(shape, 0) == (i >> log2(p.k))) & (iota(shape, 1).astype(F32) == col.reshape(1, 1, p.rows))
        ).reshape(zc * p.bcols, p.rows)
        parts = []
        for c in range(3):
            m = r_ref[:, at + 1 + c, :][:, 128 * d : 128 * d + 128]
            parts.append(jnp.concatenate([spin(jnp.broadcast_to(m[r : r + 1], (8, 128))) for r in range(n)], axis=0))
        o = select(g, jnp.concatenate(parts, axis=1))
        side = []
        for c in range(3):
            blocks = o[:, 128 * c : 128 * c + 128]
            row = [lay_out(blocks[8 * t : 8 * t + 8], 0) for t in range(zc * p.bcols // 8)]
            per = p.bcols // 8
            side.append([jnp.concatenate(row[z * per : (z + 1) * per], axis=1) for z in range(zc)])
        sides.append(side)
    return sides


def local_kernel(p, r_ref, b_ref, lo_ref, hi_ref, e_ref, next_ref, w_ref):
    n, zc = p.n, p.zc
    me = lax.axis_index("xy")
    nxt, prv = lax.rem(me + 1, n), lax.rem(me + n - 1, n)
    zero = jnp.zeros((p.ny, p.nx), F32)
    outer_u = outer_velocity(p, r_ref)
    for z in range(zc):
        e = [e_ref[c, z] for c in range(3)]
        e0, e2 = [], []
        for u, device in zip(outer_u, (nxt, prv)):
            b = [row_of(p, r_ref, device, p.ru + (c * zc + z) * p.wrap) for c in range(3)]
            e0.append(u[1][z] * b[2] - u[2][z] * b[1])
            e2.append(u[0][z] * b[1] - u[1][z] * b[0])
        above = [e_ref[c, z + 1] if z < zc - 1 else zero for c in range(2)]
        below = [e_ref[c, z - 1] if z > 0 else zero for c in range(2)]
        curl = [
            (y_next(e[2], e2[0]) - y_prev(e[2], e2[1])) - (above[1] - below[1]),
            (above[0] - below[0]) - (x_next(e[2]) - x_prev(e[2])),
            (x_next(e[1]) - x_prev(e[1])) - (y_next(e[0], e0[0]) - y_prev(e[0], e0[1])),
        ]
        for c in range(3):
            north, south = edge_rows(p, r_ref, nxt, prv, p.ru + (c * zc + z) * p.wrap)
            total = curl[c] + north + south
            if c < 2 and z == 0:
                total = total + lo_ref[c]
            if c < 2 and z == zc - 1:
                total = total + hi_ref[c]
            next_ref[c, z] = b_ref[c, z] + 0.05 * total
    half_fine = p.edge * p.edge // 2
    half_area = p.area // 2
    ex = log2(p.edge)
    c, f = iota((half_area, half_fine), 0), iota((half_area, half_fine), 1)
    coarse = ((f >> (ex + 1)) << (ex - 1)) + ((f & (p.edge - 1)) >> 1)
    sel = one_hot(coarse == c)
    sel = jnp.concatenate([sel, sel], axis=0)
    w_ref[...] = sel


def finish_kernel(p, r_ref, g_ref, w_ref, v_ref, n_ref, lo_ref, hi_ref, vel_hbm, mag_hbm, vel, mag, sems):
    zc = p.zc
    copies = []
    for z in range(zc):
        dz = [jnp.zeros((p.ny, p.nx), F32)] * 2
        outer = dz[0]
        if z == zc - 1:
            dz = [dz[c] + hi_ref[c] for c in range(2)]
            outer = outer + hi_ref[2]
        if z == 0:
            dz = [dz[c] - lo_ref[c] for c in range(2)]
            outer = outer + lo_ref[2]
        mag[0, z] = n_ref[0, z] + 0.05 * -dz[1]
        mag[1, z] = n_ref[1, z] + 0.05 * dz[0]
        mag[2, z] = n_ref[2, z] + 0.05 * outer
    copies.append(pltpu.make_async_copy(mag, mag_hbm, sems.at[3]))
    copies[-1].start()
    half_fine = p.edge * p.edge // 2
    half_area = p.area // 2
    sel = w_ref[...]
    g = g_ref[...]
    ws = [slice(h * half_area, (h + 1) * half_area) for h in range(2)]
    s = p.slots
    m = zc * s
    for c in range(3):
        hi, lo = split(r_ref[:, c * p.rc : (c + 1) * p.rc, :].reshape(p.rows, p.area) * 0.1)
        parts = dot(g, jnp.concatenate([hi, lo], axis=1)).astype(BF16)
        hi, lo = parts[:, : p.area], parts[:, p.area :]
        pairs = [jnp.concatenate([hi[:, w], lo[:, w]], axis=1) for w in ws]
        add = dot(jnp.concatenate(pairs, axis=0), sel)
        for z in range(zc):
            for h in range(2):
                fw = slice(h * half_fine, (h + 1) * half_fine)
                part = add[h * m + z * s : h * m + (z + 1) * s]
                for d in range(2):
                    vel[c, 2 * z + d, :, fw] = v_ref[c, 2 * z + d, :, fw] + part
        copies.append(pltpu.make_async_copy(vel.at[c], vel_hbm.at[c], sems.at[c]))
        copies[-1].start()
    for copy in copies:
        copy.wait()


def struct(*shape, dtype=F32):
    return jax.ShapeDtypeStruct(shape, dtype)


def call(kernel, ins, outs, scratch=(), grant=20 << 20):
    return pl.pallas_call(
        kernel,
        out_shape=[o for o, _ in outs],
        in_specs=ins,
        out_specs=[spec for _, spec in outs],
        scratch_shapes=list(scratch),
        cost_estimate=pl.CostEstimate(flops=1 << 24, bytes_accessed=1 << 20, transcendentals=0),
        compiler_params=pltpu.CompilerParams(vmem_limit_bytes=grant),
    )


def ring(axis, step):
    n = lax.axis_size(axis)
    return [(i, (i + step) % n) for i in range(n)]


def planes(up, down):
    below = lax.ppermute(up, "gz", ring("gz", 1))
    above = lax.ppermute(down, "gz", ring("gz", -1))
    return below, above


def body(velocity, magnetic, slot_block_table):
    p = Plan(velocity.shape, magnetic.shape, lax.axis_size("xy"))
    plane = (p.ny, p.nx)
    dma = pltpu.SemaphoreType.DMA
    table = slot_block_table.reshape(1, p.slots)
    sent, up, down = call(
        functools.partial(restrict_kernel, p),
        [HBM] * 3,
        [(struct(p.n, p.r1, p.area), HBM), (struct(2, *plane), HBM), (struct(2, *plane), HBM)],
        [
            pltpu.VMEM(velocity.shape, F32),
            pltpu.VMEM((1, p.slots), jnp.int32),
            pltpu.VMEM(magnetic.shape, F32),
            pltpu.VMEM((p.n, p.r1, p.area), F32),
            pltpu.VMEM((-(-p.rb // 8) * 8, p.area), F32),
            pltpu.VMEM((-(-p.rb // 8) * 8, p.area), F32),
            dma((12,)),
        ],
        ALL_VMEM,
    )(velocity, table, magnetic)
    got = lax.all_to_all(sent, "xy", 0, 0, tiled=True)
    below, above = planes(up, down)
    held, held_table, _ = lax.optimization_barrier((magnetic, table, up))
    field, current, diffused, g3 = call(
        functools.partial(interior_kernel, p),
        [VMEM] * 2,
        [(struct(*magnetic.shape), VMEM)] * 3 + [(struct(p.zc * p.slots, p.rows, dtype=BF16), VMEM)],
    )(held, held_table)
    sent, emf, up, down = call(
        functools.partial(field_kernel, p),
        [VMEM] * 5,
        [
            (struct(p.n, p.ru, p.area), VMEM),
            (struct(*magnetic.shape), VMEM),
            (struct(3, *plane), VMEM),
            (struct(3, *plane), VMEM),
        ],
    )(got, field, current, below, above)
    got_force = lax.all_to_all(sent, "xy", 0, 0, tiled=True)
    emf_below, emf_above = planes(up, down)
    partial, widen = call(
        functools.partial(local_kernel, p), [VMEM] * 5, [(struct(*magnetic.shape), VMEM), (struct(p.area, p.edge * p.edge // 2, dtype=BF16), VMEM)]
    )(got, diffused, below, above, emf)
    return tuple(
        call(
            functools.partial(finish_kernel, p),
            [VMEM] * 7,
            [(struct(*velocity.shape), HBM), (struct(*magnetic.shape), HBM)],
            [pltpu.VMEM(velocity.shape, F32), pltpu.VMEM(magnetic.shape, F32), dma((4,))],
        )(got_force, g3, widen, velocity, partial, emf_below, emf_above)
    )


def solution(mesh):
    return jax.shard_map(
        body,
        mesh=mesh,
        in_specs=(P(None, "gz", "xy", None), P(None, "gz", "xy", None), P("xy")),
        out_specs=(P(None, "gz", "xy", None), P(None, "gz", "xy", None)),
        check_vma=False,
    )
```

profile of v0, /device:TPU:0, one launch (start us, length us, event | category | flops | bytes accessed | tf_op | source)
XLA Modules:
  0.0 33.1 jit_solution(12437355624109131739)
XLA Ops:
  0.6 2.8 %shard_map.50 = (f32[8,40,256]{2,1,0:T(8,128)}, f32[2,16,512]{2,1,0:T(8,128)}, f32[2,16,512]{2,1,0:T(8,128)}) custom-call(f32[3,4,32,1024]{3,2,1,0:T(8,128)} %v_ref.1, s32[1,32]{1,0:T(1,128)} %bitcast.1, f32[3,2,16,512]{3,2,1,0:T(8,128)} %b_ref), custom_call_target="tpu_custom_call" | custom-call | flops 16777216 | bytes 1048576 | tf_op jit(solution)/shard_map/pallas_call | solution.py:480
  3.4 0.0 copy-start
  3.4 5.3 %all-to-all-start = ((f32[8,40,256]{2,1,0:T(8,128)}), f32[8,40,256]{2,1,0:T(8,128)S(1)}, u32[]{:S(2)}, u32[]{:S(2)}) async-start(f32[8,40,256]{2,1,0:T(8,128)} %get-tuple-element.17), calls=%async_computation | async-start | bytes 655360 | tf_op jit(solution)/shard_map/all_to_all | solution.py:495
  8.8 3.6 %collective-permute-start.1 = (f32[2,16,512]{2,1,0:T(8,128)}, f32[2,16,512]{2,1,0:T(8,128)S(1)}, u32[]{:S(2)}, u32[]{:S(2)}) collective-permute-start(f32[2,16,512]{2,1,0:T(8,128)} %get-tuple-element.23), channel_id=1, source_target_pairs={{0,3},{1,0},{2,1},{3,2},{4,7},{5,4},{6,5},{7,6},{8,11},{9,8},{10,9... | collective-permute-start | bytes 196616 | tf_op jit(solution)/shard_map/ppermute | solution.py:471
  12.4 0.0 collective-permute-start
  12.4 0.0 copy-start.1
  12.4 0.9 %copy-done.1 = f32[3,2,16,512]{3,2,1,0:T(8,128)S(1)} copy-done((f32[3,2,16,512]{3,2,1,0:T(8,128)S(1)}, f32[3,2,16,512]{3,2,1,0:T(8,128)}, u32[]{:S(2)}) %copy-start.1) | copy-done | bytes 196632
  13.3 0.0 copy-start.2
  13.3 0.7 %copy-done.2 = s32[32]{0:T(128)S(1)} copy-done((s32[32]{0:T(128)S(1)}, s32[32]{0:T(128)}, u32[]{:S(2)}) %copy-start.2) | copy-done | bytes 152
  14.0 0.2 shard_map.51
  14.2 1.0 %collective-permute-done.1.hi_ref = f32[2,16,512]{2,1,0:T(8,128)S(1)} collective-permute-done((f32[2,16,512]{2,1,0:T(8,128)}, f32[2,16,512]{2,1,0:T(8,128)S(1)}, u32[]{:S(2)}, u32[]{:S(2)}) %collective-permute-start.1) | collective-permute-done | bytes 65568 | tf_op jit(solution)/shard_map/ppermute | solution.py:471
  15.2 3.5 %collective-permute-done.lo_ref = f32[2,16,512]{2,1,0:T(8,128)S(1)} collective-permute-done((f32[2,16,512]{2,1,0:T(8,128)}, f32[2,16,512]{2,1,0:T(8,128)S(1)}, u32[]{:S(2)}, u32[]{:S(2)}) %collective-permute-start) | collective-permute-done | bytes 65568 | tf_op jit(solution)/shard_map/ppermute | solution.py:470
  18.7 0.0 all-to-all-done.r_ref
  18.7 1.1 %shard_map.52 = (f32[8,24,256]{2,1,0:T(8,128)}, f32[3,2,16,512]{3,2,1,0:T(8,128)S(1)}, f32[3,16,512]{2,1,0:T(8,128)S(1)}, f32[3,16,512]{2,1,0:T(8,128)S(1)}) custom-call(f32[8,40,256]{2,1,0:T(8,128)S(1)} %all-to-all-done.r_ref, f32[3,2,16,512]{3,2,1,0:T(8,128)S(1)} %get-tuple-element.21.b_ref, f32[3,2,16,512]{3,2,1,0:T(8,128)S(1)} %get-tuple-element.22.j_ref, ...), custom_call_target="tpu_custom_call" | custom-call | flops 16777216 | bytes 1048576 | tf_op jit(solution)/shard_map/pallas_call | solution.py:503
  19.8 4.2 %all-to-all-start.1 = ((f32[8,24,256]{2,1,0:T(8,128)}), f32[8,24,256]{2,1,0:T(8,128)S(1)}, u32[]{:S(2)}, u32[]{:S(2)}) async-start(f32[8,24,256]{2,1,0:T(8,128)} %get-tuple-element.24), calls=%async_computation.1 | async-start | bytes 393216 | tf_op jit(solution)/shard_map/all_to_all | solution.py:513
  24.0 0.0 collective-permute-start.2
  24.0 3.8 %collective-permute-start.3 = (f32[3,16,512]{2,1,0:T(8,128)S(1)}, f32[3,16,512]{2,1,0:T(8,128)S(1)}, u32[]{:S(2)}, u32[]{:S(2)}) collective-permute-start(f32[3,16,512]{2,1,0:T(8,128)S(1)} %get-tuple-element.31), channel_id=1, source_target_pairs={{0,3},{1,0},{2,1},{3,2},{4,7},{5,4},{6,5},{7,6},{8,11},{9,8},{10,9... | collective-permute-start | bytes 294920 | tf_op jit(solution)/shard_map/ppermute | solution.py:471
  27.8 0.4 %shard_map.53 = (f32[3,2,16,512]{3,2,1,0:T(8,128)S(1)}, bf16[256,512]{1,0:T(8,128)(2,1)S(1)}) custom-call(f32[8,40,256]{2,1,0:T(8,128)S(1)} %all-to-all-done.r_ref, f32[3,2,16,512]{3,2,1,0:T(8,128)S(1)} %get-tuple-element.26.b_ref, f32[2,16,512]{2,1,0:T(8,128)S(1)} %collective-permute-done.lo_ref, f32[2,16,512]{2,1,0:T(8,128)S(1)} %collective-permute-done.1.hi_ref, ...), custom_call_target="tpu_custom_call" | custom-call | flops 16777216 | bytes 1048576 | tf_op jit(solution)/shard_map/pallas_call | solution.py:515
  28.2 3.2 %collective-permute-done.2.lo_ref = f32[3,16,512]{2,1,0:T(8,128)S(1)} collective-permute-done((f32[3,16,512]{2,1,0:T(8,128)S(1)}, f32[3,16,512]{2,1,0:T(8,128)S(1)}, u32[]{:S(2)}, u32[]{:S(2)}) %collective-permute-start.2) | collective-permute-done | bytes 98336 | tf_op jit(solution)/shard_map/ppermute | solution.py:470
  31.4 0.0 collective-permute-done.3.hi_ref
  31.4 0.0 all-to-all-done.1.r_ref
  31.4 0.0 copy-done
  31.4 1.6 %shard_map.54 = (f32[3,4,32,1024]{3,2,1,0:T(8,128)}, f32[3,2,16,512]{3,2,1,0:T(8,128)}) custom-call(f32[8,24,256]{2,1,0:T(8,128)S(1)} %all-to-all-done.1.r_ref, bf16[64,64]{1,0:T(8,128)(2,1)S(1)} %get-tuple-element.25.g_ref, bf16[256,512]{1,0:T(8,128)(2,1)S(1)} %get-tuple-element.28.w_ref, f32[3,4,32,1024]{3,2,1,0:T(8,128)S(1)} %copy-done, ...), custom_call_target="tpu_custom_call" | custom-call | flops 16777216 | bytes 1048576 | tf_op jit(solution)/shard_map/pallas_call | solution.py:519
Async XLA Ops:
  3.4 28.0 %copy-start = (f32[3,4,32,1024]{3,2,1,0:T(8,128)S(1)}, f32[3,4,32,1024]{3,2,1,0:T(8,128)}, u32[]{:S(2)}) copy-start(f32[3,4,32,1024]{3,2,1,0:T(8,128)} %v_ref.1) | copy-start | bytes 4718596
  3.4 15.2 %all-to-all-start = ((f32[8,40,256]{2,1,0:T(8,128)}), f32[8,40,256]{2,1,0:T(8,128)S(1)}, u32[]{:S(2)}, u32[]{:S(2)}) async-start(f32[8,40,256]{2,1,0:T(8,128)} %get-tuple-element.17), calls=%async_computation | async-start | bytes 655360 | tf_op jit(solution)/shard_map/all_to_all | solution.py:495
  8.8 6.4 %collective-permute-start.1 = (f32[2,16,512]{2,1,0:T(8,128)}, f32[2,16,512]{2,1,0:T(8,128)S(1)}, u32[]{:S(2)}, u32[]{:S(2)}) collective-permute-start(f32[2,16,512]{2,1,0:T(8,128)} %get-tuple-element.23), channel_id=1, source_target_pairs={{0,3},{1,0},{2,1},{3,2},{4,7},{5,4},{6,5},{7,6},{8,11},{9,8},{10,9... | collective-permute-start | bytes 196616 | tf_op jit(solution)/shard_map/ppermute | solution.py:471
  12.4 6.3 %collective-permute-start = (f32[2,16,512]{2,1,0:T(8,128)}, f32[2,16,512]{2,1,0:T(8,128)S(1)}, u32[]{:S(2)}, u32[]{:S(2)}) collective-permute-start(f32[2,16,512]{2,1,0:T(8,128)} %get-tuple-element.18), channel_id=1, source_target_pairs={{0,1},{1,2},{2,3},{3,0},{4,5},{5,6},{6,7},{7,4},{8,9},{9,10},{10,1... | collective-permute-start | bytes 196616 | tf_op jit(solution)/shard_map/ppermute | solution.py:470
  12.4 0.9 %copy-start.1 = (f32[3,2,16,512]{3,2,1,0:T(8,128)S(1)}, f32[3,2,16,512]{3,2,1,0:T(8,128)}, u32[]{:S(2)}) copy-start(f32[3,2,16,512]{3,2,1,0:T(8,128)} %b_ref) | copy-start | bytes 589828
  13.3 0.7 %copy-start.2 = (s32[32]{0:T(128)S(1)}, s32[32]{0:T(128)}, u32[]{:S(2)}) copy-start(s32[32]{0:T(128)} %param.5) | copy-start | bytes 388
  19.8 11.7 %all-to-all-start.1 = ((f32[8,24,256]{2,1,0:T(8,128)}), f32[8,24,256]{2,1,0:T(8,128)S(1)}, u32[]{:S(2)}, u32[]{:S(2)}) async-start(f32[8,24,256]{2,1,0:T(8,128)} %get-tuple-element.24), calls=%async_computation.1 | async-start | bytes 393216 | tf_op jit(solution)/shard_map/all_to_all | solution.py:513
  24.0 7.5 %collective-permute-start.2 = (f32[3,16,512]{2,1,0:T(8,128)S(1)}, f32[3,16,512]{2,1,0:T(8,128)S(1)}, u32[]{:S(2)}, u32[]{:S(2)}) collective-permute-start(f32[3,16,512]{2,1,0:T(8,128)S(1)} %get-tuple-element.30), channel_id=1, source_target_pairs={{0,1},{1,2},{2,3},{3,0},{4,5},{5,6},{6,7},{7,4},{8,9},{9,10},{10,1... | collective-permute-start | bytes 294920 | tf_op jit(solution)/shard_map/ppermute | solution.py:470
  24.0 7.5 %collective-permute-start.3 = (f32[3,16,512]{2,1,0:T(8,128)S(1)}, f32[3,16,512]{2,1,0:T(8,128)S(1)}, u32[]{:S(2)}, u32[]{:S(2)}) collective-permute-start(f32[3,16,512]{2,1,0:T(8,128)S(1)} %get-tuple-element.31), channel_id=1, source_target_pairs={{0,3},{1,0},{2,1},{3,2},{4,7},{5,4},{6,5},{7,6},{8,11},{9,8},{10,9... | collective-permute-start | bytes 294920 | tf_op jit(solution)/shard_map/ppermute | solution.py:471
where the time goes:
time: 33.4 us; the launch traced here: 33.1 us
  starting transfers between devices  17 us (51%)
  waiting for transfers between devices  7.68 us (23%)
  Pallas kernels  6.15 us (18%)
  local copies, waits for them, and re-layouts  1.59 us (5%)
  between operations  0.68 us (2%)
    ppermute x2, starting transfers between devices, planes(): above = lax.ppermute(down, 'gz', ring('gz', -1))  7.42 us
    ppermute x2, waiting for transfers between devices, planes(): below = lax.ppermute(up, 'gz', ring('gz', 1))  6.69 us
    all_to_all x1, starting transfers between devices, body(): got = lax.all_to_all(sent, 'xy', 0, 0, tiled=True)  5.34 us
    all_to_all x1, starting transfers between devices, body(): got_force = lax.all_to_all(sent, 'xy', 0, 0, tiled=True)  4.2 us
    pallas_call x1, Pallas kernels, body(): call(functools.partial(restrict_kernel, p), [HBM] * 3, [(struct(p.n, p.r1...  2.79 us
    pallas_call x1, Pallas kernels, body(): call(functools.partial(finish_kernel, p), [VMEM] * 7, [(struct(*velocity....  1.62 us
    unnamed x6, local copies, waits for them, and re-layouts  1.59 us
    pallas_call x1, Pallas kernels, body(): call(functools.partial(field_kernel, p), [VMEM] * 5, [(struct(p.n, p.ru,...  1.1 us
  transfers between devices with their start and end apart: 6, of which 3 were waited for; matrix products, arithmetic and copies ran while one was open for 0% of the time, Pallas kernels for 2%

commit v1 on v0

--- a/solution.py
+++ b/solution.py
@@ -104,9 +104,9 @@
     b_copy = pltpu.make_async_copy(b_hbm, b_ref, sems.at[1])
     v_copies = [pltpu.make_async_copy(v_hbm.at[c], v_ref.at[c], sems.at[2 + c]) for c in range(3)]
     t_copy.start()
+    b_copy.start()
     for copy in v_copies:
         copy.start()
-    b_copy.start()
     half_fine = p.edge * p.edge // 2
     half_area = p.area // 2
     f, c = iota((half_fine, half_area), 0), iota((half_fine, half_area), 1)
@@ -138,17 +138,6 @@
         out[r, at : at + 1, :128] = cols[r : r + 1, :128]
         outer = jnp.where(iota((1, 128), 1) < 64, cols[north : north + 1, 128:], cols[south : south + 1, 128:])
         out[r, at : at + 1, 128:] = outer
-    averages = []
-    m = zc * s
-    ws = [slice(h * half_fine, (h + 1) * half_fine) for h in range(2)]
-    for c in range(3):
-        v_copies[c].wait()
-        u = []
-        for w in ws:
-            z_sum = [v_ref[c, 2 * z, :, w] + v_ref[c, 2 * z + 1, :, w] for z in range(zc)]
-            o = dot(jnp.concatenate(split(jnp.concatenate(z_sum, axis=0)), axis=0), sel)
-            u.append(o[:m] + o[m:])
-        averages.append(jnp.concatenate(u, axis=1) * 0.125)
     b_copy.wait()
     sends = [
         pltpu.make_async_copy(b_ref.at[0:2, zc - 1], up_hbm, sems.at[5]),
@@ -168,6 +157,16 @@
     sends.append(pltpu.make_async_copy(out.at[:, early, :], out_hbm.at[:, early, :], sems.at[7]))
     for send in sends:
         send.start()
+    averages = []
+    m = zc * s
+    ws = [slice(h * half_fine, (h + 1) * half_fine) for h in range(2)]
+    for c in range(3):
+        v_copies[c].wait()
+        z_sum = jnp.concatenate([v_ref[c, 2 * z] + v_ref[c, 2 * z + 1] for z in range(zc)], axis=0)
+        hi, lo = split(z_sum)
+        o = dot(jnp.concatenate([x[:, w] for w in ws for x in (hi, lo)], axis=0), sel)
+        u = [o[2 * h * m : (2 * h + 1) * m] + o[(2 * h + 1) * m : (2 * h + 2) * m] for h in range(2)]
+        averages.append(jnp.concatenate(u, axis=1) * 0.125)
     for c in range(3):
         blocks = select(g, averages[c])
         out[:, c * p.rc : (c + 1) * p.rc, :] = blocks.reshape(n, p.rc, p.area)

time: 33.4 us -> 33.4 us (level)
  no operation moved by 1% of the time
where the time goes in v1:
time: 33.4 us; the launch traced here: 33.1 us
  starting transfers between devices  17 us (51%)
  waiting for transfers between devices  7.68 us (23%)
  Pallas kernels  6.16 us (18%)
  local copies, waits for them, and re-layouts  1.59 us (5%)
  between operations  0.68 us (2%)
    ppermute x2, starting transfers between devices, planes(): above = lax.ppermute(down, 'gz', ring('gz', -1))  7.42 us
    ppermute x2, waiting for transfers between devices, planes(): below = lax.ppermute(up, 'gz', ring('gz', 1))  6.69 us
    all_to_all x1, starting transfers between devices, body(): got = lax.all_to_all(sent, 'xy', 0, 0, tiled=True)  5.34 us
    all_to_all x1, starting transfers between devices, body(): got_force = lax.all_to_all(sent, 'xy', 0, 0, tiled=True)  4.2 us
    pallas_call x1, Pallas kernels, body(): call(functools.partial(restrict_kernel, p), [HBM] * 3, [(struct(p.n, p.r1...  2.8 us
    pallas_call x1, Pallas kernels, body(): call(functools.partial(finish_kernel, p), [VMEM] * 7, [(struct(*velocity....  1.62 us
    unnamed x6, local copies, waits for them, and re-layouts  1.59 us
    pallas_call x1, Pallas kernels, body(): call(functools.partial(field_kernel, p), [VMEM] * 5, [(struct(p.n, p.ru,...  1.1 us
  transfers between devices with their start and end apart: 6, of which 3 were waited for; matrix products, arithmetic and copies ran while one was open for 0% of the time, Pallas kernels for 2%

profile of v1, /device:TPU:0, one launch (start us, length us, event | category | flops | bytes accessed | tf_op | source)
XLA Modules:
  0.0 33.1 jit_solution(16884479212412253889)
XLA Ops:
  0.6 2.8 %shard_map.50 = (f32[8,40,256]{2,1,0:T(8,128)}, f32[2,16,512]{2,1,0:T(8,128)}, f32[2,16,512]{2,1,0:T(8,128)}) custom-call(f32[3,4,32,1024]{3,2,1,0:T(8,128)} %v_ref.1, s32[1,32]{1,0:T(1,128)} %bitcast.1, f32[3,2,16,512]{3,2,1,0:T(8,128)} %b_ref), custom_call_target="tpu_custom_call" | custom-call | flops 16777216 | bytes 1048576 | tf_op jit(solution)/shard_map/pallas_call | solution.py:479
  3.4 0.0 copy-start
  3.4 5.3 %all-to-all-start = ((f32[8,40,256]{2,1,0:T(8,128)}), f32[8,40,256]{2,1,0:T(8,128)S(1)}, u32[]{:S(2)}, u32[]{:S(2)}) async-start(f32[8,40,256]{2,1,0:T(8,128)} %get-tuple-element.17), calls=%async_computation | async-start | bytes 655360 | tf_op jit(solution)/shard_map/all_to_all | solution.py:494
  8.8 3.6 %collective-permute-start.1 = (f32[2,16,512]{2,1,0:T(8,128)}, f32[2,16,512]{2,1,0:T(8,128)S(1)}, u32[]{:S(2)}, u32[]{:S(2)}) collective-permute-start(f32[2,16,512]{2,1,0:T(8,128)} %get-tuple-element.23), channel_id=1, source_target_pairs={{0,3},{1,0},{2,1},{3,2},{4,7},{5,4},{6,5},{7,6},{8,11},{9,8},{10,9... | collective-permute-start | bytes 196616 | tf_op jit(solution)/shard_map/ppermute | solution.py:470
  12.4 0.0 collective-permute-start
  12.4 0.0 copy-start.1
  12.4 0.9 %copy-done.1 = f32[3,2,16,512]{3,2,1,0:T(8,128)S(1)} copy-done((f32[3,2,16,512]{3,2,1,0:T(8,128)S(1)}, f32[3,2,16,512]{3,2,1,0:T(8,128)}, u32[]{:S(2)}) %copy-start.1) | copy-done | bytes 196632
  13.3 0.0 copy-start.2
  13.3 0.7 %copy-done.2 = s32[32]{0:T(128)S(1)} copy-done((s32[32]{0:T(128)S(1)}, s32[32]{0:T(128)}, u32[]{:S(2)}) %copy-start.2) | copy-done | bytes 152
  14.0 0.2 shard_map.51
  14.2 1.0 %collective-permute-done.1.hi_ref = f32[2,16,512]{2,1,0:T(8,128)S(1)} collective-permute-done((f32[2,16,512]{2,1,0:T(8,128)}, f32[2,16,512]{2,1,0:T(8,128)S(1)}, u32[]{:S(2)}, u32[]{:S(2)}) %collective-permute-start.1) | collective-permute-done | bytes 65568 | tf_op jit(solution)/shard_map/ppermute | solution.py:470
  15.2 3.5 %collective-permute-done.lo_ref = f32[2,16,512]{2,1,0:T(8,128)S(1)} collective-permute-done((f32[2,16,512]{2,1,0:T(8,128)}, f32[2,16,512]{2,1,0:T(8,128)S(1)}, u32[]{:S(2)}, u32[]{:S(2)}) %collective-permute-start) | collective-permute-done | bytes 65568 | tf_op jit(solution)/shard_map/ppermute | solution.py:469
  18.7 0.0 all-to-all-done.r_ref
  18.7 1.1 %shard_map.52 = (f32[8,24,256]{2,1,0:T(8,128)}, f32[3,2,16,512]{3,2,1,0:T(8,128)S(1)}, f32[3,16,512]{2,1,0:T(8,128)S(1)}, f32[3,16,512]{2,1,0:T(8,128)S(1)}) custom-call(f32[8,40,256]{2,1,0:T(8,128)S(1)} %all-to-all-done.r_ref, f32[3,2,16,512]{3,2,1,0:T(8,128)S(1)} %get-tuple-element.21.b_ref, f32[3,2,16,512]{3,2,1,0:T(8,128)S(1)} %get-tuple-element.22.j_ref, ...), custom_call_target="tpu_custom_call" | custom-call | flops 16777216 | bytes 1048576 | tf_op jit(solution)/shard_map/pallas_call | solution.py:502
  19.8 4.2 %all-to-all-start.1 = ((f32[8,24,256]{2,1,0:T(8,128)}), f32[8,24,256]{2,1,0:T(8,128)S(1)}, u32[]{:S(2)}, u32[]{:S(2)}) async-start(f32[8,24,256]{2,1,0:T(8,128)} %get-tuple-element.24), calls=%async_computation.1 | async-start | bytes 393216 | tf_op jit(solution)/shard_map/all_to_all | solution.py:512
  24.0 0.0 collective-permute-start.2
  24.0 3.8 %collective-permute-start.3 = (f32[3,16,512]{2,1,0:T(8,128)S(1)}, f32[3,16,512]{2,1,0:T(8,128)S(1)}, u32[]{:S(2)}, u32[]{:S(2)}) collective-permute-start(f32[3,16,512]{2,1,0:T(8,128)S(1)} %get-tuple-element.31), channel_id=1, source_target_pairs={{0,3},{1,0},{2,1},{3,2},{4,7},{5,4},{6,5},{7,6},{8,11},{9,8},{10,9... | collective-permute-start | bytes 294920 | tf_op jit(solution)/shard_map/ppermute | solution.py:470
  27.8 0.4 %shard_map.53 = (f32[3,2,16,512]{3,2,1,0:T(8,128)S(1)}, bf16[256,512]{1,0:T(8,128)(2,1)S(1)}) custom-call(f32[8,40,256]{2,1,0:T(8,128)S(1)} %all-to-all-done.r_ref, f32[3,2,16,512]{3,2,1,0:T(8,128)S(1)} %get-tuple-element.26.b_ref, f32[2,16,512]{2,1,0:T(8,128)S(1)} %collective-permute-done.lo_ref, f32[2,16,512]{2,1,0:T(8,128)S(1)} %collective-permute-done.1.hi_ref, ...), custom_call_target="tpu_custom_call" | custom-call | flops 16777216 | bytes 1048576 | tf_op jit(solution)/shard_map/pallas_call | solution.py:514
  28.2 3.2 %collective-permute-done.2.lo_ref = f32[3,16,512]{2,1,0:T(8,128)S(1)} collective-permute-done((f32[3,16,512]{2,1,0:T(8,128)S(1)}, f32[3,16,512]{2,1,0:T(8,128)S(1)}, u32[]{:S(2)}, u32[]{:S(2)}) %collective-permute-start.2) | collective-permute-done | bytes 98336 | tf_op jit(solution)/shard_map/ppermute | solution.py:469
  31.4 0.0 collective-permute-done.3.hi_ref
  31.4 0.0 all-to-all-done.1.r_ref
  31.4 0.0 copy-done
  31.5 1.6 %shard_map.54 = (f32[3,4,32,1024]{3,2,1,0:T(8,128)}, f32[3,2,16,512]{3,2,1,0:T(8,128)}) custom-call(f32[8,24,256]{2,1,0:T(8,128)S(1)} %all-to-all-done.1.r_ref, bf16[64,64]{1,0:T(8,128)(2,1)S(1)} %get-tuple-element.25.g_ref, bf16[256,512]{1,0:T(8,128)(2,1)S(1)} %get-tuple-element.28.w_ref, f32[3,4,32,1024]{3,2,1,0:T(8,128)S(1)} %copy-done, ...), custom_call_target="tpu_custom_call" | custom-call | flops 16777216 | bytes 1048576 | tf_op jit(solution)/shard_map/pallas_call | solution.py:518
Async XLA Ops:
  3.4 28.0 %copy-start = (f32[3,4,32,1024]{3,2,1,0:T(8,128)S(1)}, f32[3,4,32,1024]{3,2,1,0:T(8,128)}, u32[]{:S(2)}) copy-start(f32[3,4,32,1024]{3,2,1,0:T(8,128)} %v_ref.1) | copy-start | bytes 4718596
  3.4 15.2 %all-to-all-start = ((f32[8,40,256]{2,1,0:T(8,128)}), f32[8,40,256]{2,1,0:T(8,128)S(1)}, u32[]{:S(2)}, u32[]{:S(2)}) async-start(f32[8,40,256]{2,1,0:T(8,128)} %get-tuple-element.17), calls=%async_computation | async-start | bytes 655360 | tf_op jit(solution)/shard_map/all_to_all | solution.py:494
  8.8 6.4 %collective-permute-start.1 = (f32[2,16,512]{2,1,0:T(8,128)}, f32[2,16,512]{2,1,0:T(8,128)S(1)}, u32[]{:S(2)}, u32[]{:S(2)}) collective-permute-start(f32[2,16,512]{2,1,0:T(8,128)} %get-tuple-element.23), channel_id=1, source_target_pairs={{0,3},{1,0},{2,1},{3,2},{4,7},{5,4},{6,5},{7,6},{8,11},{9,8},{10,9... | collective-permute-start | bytes 196616 | tf_op jit(solution)/shard_map/ppermute | solution.py:470
  12.4 6.3 %collective-permute-start = (f32[2,16,512]{2,1,0:T(8,128)}, f32[2,16,512]{2,1,0:T(8,128)S(1)}, u32[]{:S(2)}, u32[]{:S(2)}) collective-permute-start(f32[2,16,512]{2,1,0:T(8,128)} %get-tuple-element.18), channel_id=1, source_target_pairs={{0,1},{1,2},{2,3},{3,0},{4,5},{5,6},{6,7},{7,4},{8,9},{9,10},{10,1... | collective-permute-start | bytes 196616 | tf_op jit(solution)/shard_map/ppermute | solution.py:469
  12.4 0.9 %copy-start.1 = (f32[3,2,16,512]{3,2,1,0:T(8,128)S(1)}, f32[3,2,16,512]{3,2,1,0:T(8,128)}, u32[]{:S(2)}) copy-start(f32[3,2,16,512]{3,2,1,0:T(8,128)} %b_ref) | copy-start | bytes 589828
  13.3 0.7 %copy-start.2 = (s32[32]{0:T(128)S(1)}, s32[32]{0:T(128)}, u32[]{:S(2)}) copy-start(s32[32]{0:T(128)} %param.5) | copy-start | bytes 388
  19.8 11.7 %all-to-all-start.1 = ((f32[8,24,256]{2,1,0:T(8,128)}), f32[8,24,256]{2,1,0:T(8,128)S(1)}, u32[]{:S(2)}, u32[]{:S(2)}) async-start(f32[8,24,256]{2,1,0:T(8,128)} %get-tuple-element.24), calls=%async_computation.1 | async-start | bytes 393216 | tf_op jit(solution)/shard_map/all_to_all | solution.py:512
  24.0 7.5 %collective-permute-start.2 = (f32[3,16,512]{2,1,0:T(8,128)S(1)}, f32[3,16,512]{2,1,0:T(8,128)S(1)}, u32[]{:S(2)}, u32[]{:S(2)}) collective-permute-start(f32[3,16,512]{2,1,0:T(8,128)S(1)} %get-tuple-element.30), channel_id=1, source_target_pairs={{0,1},{1,2},{2,3},{3,0},{4,5},{5,6},{6,7},{7,4},{8,9},{9,10},{10,1... | collective-permute-start | bytes 294920 | tf_op jit(solution)/shard_map/ppermute | solution.py:469
  24.0 7.5 %collective-permute-start.3 = (f32[3,16,512]{2,1,0:T(8,128)S(1)}, f32[3,16,512]{2,1,0:T(8,128)S(1)}, u32[]{:S(2)}, u32[]{:S(2)}) collective-permute-start(f32[3,16,512]{2,1,0:T(8,128)S(1)} %get-tuple-element.31), channel_id=1, source_target_pairs={{0,3},{1,0},{2,1},{3,2},{4,7},{5,4},{6,5},{7,6},{8,11},{9,8},{10,9... | collective-permute-start | bytes 294920 | tf_op jit(solution)/shard_map/ppermute | solution.py:470

commit v2 on v1

--- a/solution.py
+++ b/solution.py
@@ -417,7 +417,7 @@
         mag[0, z] = n_ref[0, z] + 0.05 * -dz[1]
         mag[1, z] = n_ref[1, z] + 0.05 * dz[0]
         mag[2, z] = n_ref[2, z] + 0.05 * outer
-    copies.append(pltpu.make_async_copy(mag, mag_hbm, sems.at[3]))
+    copies.append(pltpu.make_async_copy(mag, mag_hbm, sems.at[0]))
     copies[-1].start()
     half_fine = p.edge * p.edge // 2
     half_area = p.area // 2
@@ -438,8 +438,9 @@
                 part = add[h * m + z * s : h * m + (z + 1) * s]
                 for d in range(2):
                     vel[c, 2 * z + d, :, fw] = v_ref[c, 2 * z + d, :, fw] + part
-        copies.append(pltpu.make_async_copy(vel.at[c], vel_hbm.at[c], sems.at[c]))
-        copies[-1].start()
+            fine = pl.ds(2 * z, 2)
+            copies.append(pltpu.make_async_copy(vel.at[c, fine], vel_hbm.at[c, fine], sems.at[1 + c * zc + z]))
+            copies[-1].start()
     for copy in copies:
         copy.wait()
 
@@ -519,7 +520,7 @@
             functools.partial(finish_kernel, p),
             [VMEM] * 7,
             [(struct(*velocity.shape), HBM), (struct(*magnetic.shape), HBM)],
-            [pltpu.VMEM(velocity.shape, F32), pltpu.VMEM(magnetic.shape, F32), dma((4,))],
+            [pltpu.VMEM(velocity.shape, F32), pltpu.VMEM(magnetic.shape, F32), dma((1 + 3 * p.zc,))],
         )(got_force, g3, widen, velocity, partial, emf_below, emf_above)
     )
 

time: 33.4 us -> 33.3 us (level)
  no operation moved by 1% of the time
where the time goes in v2:
time: 33.3 us; the launch traced here: 32.9 us
  starting transfers between devices  17 us (51%)
  waiting for transfers between devices  7.68 us (23%)
  Pallas kernels  6.03 us (18%)
  local copies, waits for them, and re-layouts  1.59 us (5%)
  between operations  0.68 us (2%)
    ppermute x2, starting transfers between devices, planes(): above = lax.ppermute(down, 'gz', ring('gz', -1))  7.42 us
    ppermute x2, waiting for transfers between devices, planes(): below = lax.ppermute(up, 'gz', ring('gz', 1))  6.69 us
    all_to_all x1, starting transfers between devices, body(): got = lax.all_to_all(sent, 'xy', 0, 0, tiled=True)  5.34 us
    all_to_all x1, starting transfers between devices, body(): got_force = lax.all_to_all(sent, 'xy', 0, 0, tiled=True)  4.2 us
    pallas_call x1, Pallas kernels, body(): call(functools.partial(restrict_kernel, p), [HBM] * 3, [(struct(p.n, p.r1...  2.8 us
    unnamed x6, local copies, waits for them, and re-layouts  1.59 us
    pallas_call x1, Pallas kernels, body(): call(functools.partial(finish_kernel, p), [VMEM] * 7, [(struct(*velocity....  1.49 us
    pallas_call x1, Pallas kernels, body(): call(functools.partial(field_kernel, p), [VMEM] * 5, [(struct(p.n, p.ru,...  1.1 us
  transfers between devices with their start and end apart: 6, of which 3 were waited for; matrix products, arithmetic and copies ran while one was open for 0% of the time, Pallas kernels for 2%

profile of v2, /device:TPU:0, one launch (start us, length us, event | category | flops | bytes accessed | tf_op | source)
XLA Modules:
  0.0 32.9 jit_solution(7196073565151786085)
XLA Ops:
  0.6 2.8 %shard_map.50 = (f32[8,40,256]{2,1,0:T(8,128)}, f32[2,16,512]{2,1,0:T(8,128)}, f32[2,16,512]{2,1,0:T(8,128)}) custom-call(f32[3,4,32,1024]{3,2,1,0:T(8,128)} %v_ref.1, s32[1,32]{1,0:T(1,128)} %bitcast.1, f32[3,2,16,512]{3,2,1,0:T(8,128)} %b_ref), custom_call_target="tpu_custom_call" | custom-call | flops 16777216 | bytes 1048576 | tf_op jit(solution)/shard_map/pallas_call | solution.py:480
  3.4 0.0 copy-start
  3.4 5.3 %all-to-all-start = ((f32[8,40,256]{2,1,0:T(8,128)}), f32[8,40,256]{2,1,0:T(8,128)S(1)}, u32[]{:S(2)}, u32[]{:S(2)}) async-start(f32[8,40,256]{2,1,0:T(8,128)} %get-tuple-element.17), calls=%async_computation | async-start | bytes 655360 | tf_op jit(solution)/shard_map/all_to_all | solution.py:495
  8.8 3.6 %collective-permute-start.1 = (f32[2,16,512]{2,1,0:T(8,128)}, f32[2,16,512]{2,1,0:T(8,128)S(1)}, u32[]{:S(2)}, u32[]{:S(2)}) collective-permute-start(f32[2,16,512]{2,1,0:T(8,128)} %get-tuple-element.23), channel_id=1, source_target_pairs={{0,3},{1,0},{2,1},{3,2},{4,7},{5,4},{6,5},{7,6},{8,11},{9,8},{10,9... | collective-permute-start | bytes 196616 | tf_op jit(solution)/shard_map/ppermute | solution.py:471
  12.4 0.0 collective-permute-start
  12.4 0.0 copy-start.1
  12.4 0.9 %copy-done.1 = f32[3,2,16,512]{3,2,1,0:T(8,128)S(1)} copy-done((f32[3,2,16,512]{3,2,1,0:T(8,128)S(1)}, f32[3,2,16,512]{3,2,1,0:T(8,128)}, u32[]{:S(2)}) %copy-start.1) | copy-done | bytes 196632
  13.3 0.0 copy-start.2
  13.3 0.7 %copy-done.2 = s32[32]{0:T(128)S(1)} copy-done((s32[32]{0:T(128)S(1)}, s32[32]{0:T(128)}, u32[]{:S(2)}) %copy-start.2) | copy-done | bytes 152
  14.0 0.2 shard_map.51
  14.2 1.0 %collective-permute-done.1.hi_ref = f32[2,16,512]{2,1,0:T(8,128)S(1)} collective-permute-done((f32[2,16,512]{2,1,0:T(8,128)}, f32[2,16,512]{2,1,0:T(8,128)S(1)}, u32[]{:S(2)}, u32[]{:S(2)}) %collective-permute-start.1) | collective-permute-done | bytes 65568 | tf_op jit(solution)/shard_map/ppermute | solution.py:471
  15.2 3.5 %collective-permute-done.lo_ref = f32[2,16,512]{2,1,0:T(8,128)S(1)} collective-permute-done((f32[2,16,512]{2,1,0:T(8,128)}, f32[2,16,512]{2,1,0:T(8,128)S(1)}, u32[]{:S(2)}, u32[]{:S(2)}) %collective-permute-start) | collective-permute-done | bytes 65568 | tf_op jit(solution)/shard_map/ppermute | solution.py:470
  18.7 0.0 all-to-all-done.r_ref
  18.7 1.1 %shard_map.52 = (f32[8,24,256]{2,1,0:T(8,128)}, f32[3,2,16,512]{3,2,1,0:T(8,128)S(1)}, f32[3,16,512]{2,1,0:T(8,128)S(1)}, f32[3,16,512]{2,1,0:T(8,128)S(1)}) custom-call(f32[8,40,256]{2,1,0:T(8,128)S(1)} %all-to-all-done.r_ref, f32[3,2,16,512]{3,2,1,0:T(8,128)S(1)} %get-tuple-element.21.b_ref, f32[3,2,16,512]{3,2,1,0:T(8,128)S(1)} %get-tuple-element.22.j_ref, ...), custom_call_target="tpu_custom_call" | custom-call | flops 16777216 | bytes 1048576 | tf_op jit(solution)/shard_map/pallas_call | solution.py:503
  19.8 4.2 %all-to-all-start.1 = ((f32[8,24,256]{2,1,0:T(8,128)}), f32[8,24,256]{2,1,0:T(8,128)S(1)}, u32[]{:S(2)}, u32[]{:S(2)}) async-start(f32[8,24,256]{2,1,0:T(8,128)} %get-tuple-element.24), calls=%async_computation.1 | async-start | bytes 393216 | tf_op jit(solution)/shard_map/all_to_all | solution.py:513
  24.0 0.0 collective-permute-start.2
  24.0 3.8 %collective-permute-start.3 = (f32[3,16,512]{2,1,0:T(8,128)S(1)}, f32[3,16,512]{2,1,0:T(8,128)S(1)}, u32[]{:S(2)}, u32[]{:S(2)}) collective-permute-start(f32[3,16,512]{2,1,0:T(8,128)S(1)} %get-tuple-element.31), channel_id=1, source_target_pairs={{0,3},{1,0},{2,1},{3,2},{4,7},{5,4},{6,5},{7,6},{8,11},{9,8},{10,9... | collective-permute-start | bytes 294920 | tf_op jit(solution)/shard_map/ppermute | solution.py:471
  27.8 0.4 %shard_map.53 = (f32[3,2,16,512]{3,2,1,0:T(8,128)S(1)}, bf16[256,512]{1,0:T(8,128)(2,1)S(1)}) custom-call(f32[8,40,256]{2,1,0:T(8,128)S(1)} %all-to-all-done.r_ref, f32[3,2,16,512]{3,2,1,0:T(8,128)S(1)} %get-tuple-element.26.b_ref, f32[2,16,512]{2,1,0:T(8,128)S(1)} %collective-permute-done.lo_ref, f32[2,16,512]{2,1,0:T(8,128)S(1)} %collective-permute-done.1.hi_ref, ...), custom_call_target="tpu_custom_call" | custom-call | flops 16777216 | bytes 1048576 | tf_op jit(solution)/shard_map/pallas_call | solution.py:515
  28.2 3.2 %collective-permute-done.2.lo_ref = f32[3,16,512]{2,1,0:T(8,128)S(1)} collective-permute-done((f32[3,16,512]{2,1,0:T(8,128)S(1)}, f32[3,16,512]{2,1,0:T(8,128)S(1)}, u32[]{:S(2)}, u32[]{:S(2)}) %collective-permute-start.2) | collective-permute-done | bytes 98336 | tf_op jit(solution)/shard_map/ppermute | solution.py:470
  31.4 0.0 collective-permute-done.3.hi_ref
  31.4 0.0 all-to-all-done.1.r_ref
  31.4 0.0 copy-done
  31.5 1.5 %shard_map.54 = (f32[3,4,32,1024]{3,2,1,0:T(8,128)}, f32[3,2,16,512]{3,2,1,0:T(8,128)}) custom-call(f32[8,24,256]{2,1,0:T(8,128)S(1)} %all-to-all-done.1.r_ref, bf16[64,64]{1,0:T(8,128)(2,1)S(1)} %get-tuple-element.25.g_ref, bf16[256,512]{1,0:T(8,128)(2,1)S(1)} %get-tuple-element.28.w_ref, f32[3,4,32,1024]{3,2,1,0:T(8,128)S(1)} %copy-done, ...), custom_call_target="tpu_custom_call" | custom-call | flops 16777216 | bytes 1048576 | tf_op jit(solution)/shard_map/pallas_call | solution.py:519
Async XLA Ops:
  3.4 28.0 %copy-start = (f32[3,4,32,1024]{3,2,1,0:T(8,128)S(1)}, f32[3,4,32,1024]{3,2,1,0:T(8,128)}, u32[]{:S(2)}) copy-start(f32[3,4,32,1024]{3,2,1,0:T(8,128)} %v_ref.1) | copy-start | bytes 4718596
  3.4 15.2 %all-to-all-start = ((f32[8,40,256]{2,1,0:T(8,128)}), f32[8,40,256]{2,1,0:T(8,128)S(1)}, u32[]{:S(2)}, u32[]{:S(2)}) async-start(f32[8,40,256]{2,1,0:T(8,128)} %get-tuple-element.17), calls=%async_computation | async-start | bytes 655360 | tf_op jit(solution)/shard_map/all_to_all | solution.py:495
  8.8 6.4 %collective-permute-start.1 = (f32[2,16,512]{2,1,0:T(8,128)}, f32[2,16,512]{2,1,0:T(8,128)S(1)}, u32[]{:S(2)}, u32[]{:S(2)}) collective-permute-start(f32[2,16,512]{2,1,0:T(8,128)} %get-tuple-element.23), channel_id=1, source_target_pairs={{0,3},{1,0},{2,1},{3,2},{4,7},{5,4},{6,5},{7,6},{8,11},{9,8},{10,9... | collective-permute-start | bytes 196616 | tf_op jit(solution)/shard_map/ppermute | solution.py:471
  12.4 6.3 %collective-permute-start = (f32[2,16,512]{2,1,0:T(8,128)}, f32[2,16,512]{2,1,0:T(8,128)S(1)}, u32[]{:S(2)}, u32[]{:S(2)}) collective-permute-start(f32[2,16,512]{2,1,0:T(8,128)} %get-tuple-element.18), channel_id=1, source_target_pairs={{0,1},{1,2},{2,3},{3,0},{4,5},{5,6},{6,7},{7,4},{8,9},{9,10},{10,1... | collective-permute-start | bytes 196616 | tf_op jit(solution)/shard_map/ppermute | solution.py:470
  12.4 0.9 %copy-start.1 = (f32[3,2,16,512]{3,2,1,0:T(8,128)S(1)}, f32[3,2,16,512]{3,2,1,0:T(8,128)}, u32[]{:S(2)}) copy-start(f32[3,2,16,512]{3,2,1,0:T(8,128)} %b_ref) | copy-start | bytes 589828
  13.3 0.7 %copy-start.2 = (s32[32]{0:T(128)S(1)}, s32[32]{0:T(128)}, u32[]{:S(2)}) copy-start(s32[32]{0:T(128)} %param.5) | copy-start | bytes 388
  19.8 11.7 %all-to-all-start.1 = ((f32[8,24,256]{2,1,0:T(8,128)}), f32[8,24,256]{2,1,0:T(8,128)S(1)}, u32[]{:S(2)}, u32[]{:S(2)}) async-start(f32[8,24,256]{2,1,0:T(8,128)} %get-tuple-element.24), calls=%async_computation.1 | async-start | bytes 393216 | tf_op jit(solution)/shard_map/all_to_all | solution.py:513
  24.0 7.5 %collective-permute-start.2 = (f32[3,16,512]{2,1,0:T(8,128)S(1)}, f32[3,16,512]{2,1,0:T(8,128)S(1)}, u32[]{:S(2)}, u32[]{:S(2)}) collective-permute-start(f32[3,16,512]{2,1,0:T(8,128)S(1)} %get-tuple-element.30), channel_id=1, source_target_pairs={{0,1},{1,2},{2,3},{3,0},{4,5},{5,6},{6,7},{7,4},{8,9},{9,10},{10,1... | collective-permute-start | bytes 294920 | tf_op jit(solution)/shard_map/ppermute | solution.py:470
  24.0 7.5 %collective-permute-start.3 = (f32[3,16,512]{2,1,0:T(8,128)S(1)}, f32[3,16,512]{2,1,0:T(8,128)S(1)}, u32[]{:S(2)}, u32[]{:S(2)}) collective-permute-start(f32[3,16,512]{2,1,0:T(8,128)S(1)} %get-tuple-element.31), channel_id=1, source_target_pairs={{0,3},{1,0},{2,1},{3,2},{4,7},{5,4},{6,5},{7,6},{8,11},{9,8},{10,9... | collective-permute-start | bytes 294920 | tf_op jit(solution)/shard_map/ppermute | solution.py:471
